TPU v7x, 32 devices: a whole 2x2x4 slice. The times are simulated.
32 devices in a mesh: gx: 8 (over y, x, core), gy: 4 (over z).
Axes of the slice: x: 2, y: 2, z: 4, core: 2. Of those that a mesh axis runs over, the one named last changes fastest.
Arguments:
- control: float32 [4, 128, 128, 128], P(None, 'gy', 'gx'), may hold values from -6 to 6
- level_rate: float32 [4, 128], replicated, may hold values from 0.02 to 0.3
- x_rate: float32 [128], replicated, may hold values from 0.00125 to 0.01875
- y_rate: float32 [128], replicated, may hold values from 0.000625 to 0.009375
- jacobian: float32 [4, 128, 616], replicated, may hold values from -0.25 to 0.25
- innovation: float32 [4096, 616], P(('gx', 'gy')), may hold values from -8 to 8
- predictors: float32 [4096, 8], P(('gx', 'gy')), may hold values from -12 to 12
- bias_coef: float32 [8, 616], replicated, may hold values from -1.8 to 1.8
- inv_var: float32 [616], replicated, may hold values from 0.25 to 4
- obs_tile: int32 [4096, 1], P(('gx', 'gy')), may hold values from 0 to 3; in each aligned block of 128 rows (0 to 127, 128 to 255, ...) at most 32 rows name the same one
- obs_cell: int32 [4096], P(('gx', 'gy')), may hold values from 0 to 511
Outputs:
- obs_gradient: float32 [4, 128, 128, 128], P(None, 'gy', 'gx')
- departures: float32 [4096, 616], P(('gx', 'gy'))
- bias_gradient: float32 [8, 616], replicated
- obs_cost: float32 [], replicated
Inputs may be any that keep to these rules, and one draw needn't show every extreme that they name: `obs_tile`: among the 128 observations of one device at most 32 lie in the same latitude tile, and some tile holds exactly 32 of them. `obs_cell`: index of the column within the tile, row by row over 32 rows of 16 columns.
All inputs are finite; a program needn't handle non-finite values.
Results may differ from a plain program's by a relative error of at most 0.000076.
Values sent between devices are 32-bit elements; how exact they have to be, the bound alone decides.
A program may use at most 64 MiB of HBM per device.

v0:
```python
import jax
import jax.numpy as jnp
from jax import lax
from jax.sharding import PartitionSpec as P

exact_result = lax.Precision.HIGHEST


def filter_matrix(log_sums, scales):
    spread = log_sums[:, None] - log_sums[None, :]
    rows_at = lax.broadcasted_iota(jnp.int32, spread.shape, 0)
    cols_at = lax.broadcasted_iota(jnp.int32, spread.shape, 1)
    return jnp.where(rows_at >= cols_at, jnp.exp(jnp.minimum(spread, 0.0)), 0.0) * scales[None, :]


def line_terms(rates):
    decays = 1.0 - rates
    log_sums = jnp.cumsum(jnp.log(decays), axis=-1)
    scales = jnp.sqrt(1.0 - decays * decays)
    return (log_sums, scales)


def x_transposed(state, x_rate, adjoint):
    log_sums, scales = line_terms(x_rate)
    matrix = filter_matrix(log_sums, scales)
    line_data = lax.all_to_all(state, "gx", split_axis=1, concat_axis=2, tiled=True)
    pattern = "ji,vyjl->vyil" if adjoint else "ij,vyjl->vyil"
    filtered = jnp.einsum(pattern, matrix, line_data, precision=exact_result)
    return lax.all_to_all(filtered, "gx", split_axis=2, concat_axis=1, tiled=True)


def y_transposed(state, y_rate, adjoint):
    log_sums, scales = line_terms(y_rate)
    matrix = filter_matrix(log_sums, scales)
    line_data = lax.all_to_all(state, "gy", split_axis=2, concat_axis=1, tiled=True)
    pattern = "ji,vjxl->vixl" if adjoint else "ij,vjxl->vixl"
    filtered = jnp.einsum(pattern, matrix, line_data, precision=exact_result)
    return lax.all_to_all(filtered, "gy", split_axis=1, concat_axis=2, tiled=True)


def x_filter(state, x_rate, adjoint):
    return x_transposed(state, x_rate, adjoint)


def y_filter(state, y_rate, adjoint):
    return y_transposed(state, y_rate, adjoint)


def level_filter(state, level_rate, adjoint):
    log_sums, scales = line_terms(level_rate)
    matrices = jax.vmap(filter_matrix)(log_sums, scales)
    pattern = "vml,vyxm->vyxl" if adjoint else "vml,vyxl->vyxm"
    return jnp.einsum(pattern, matrices, state, precision=exact_result)


def shards(
    control,
    level_rate,
    x_rate,
    y_rate,
    jacobian,
    innovation,
    predictors,
    bias_coef,
    inv_var,
    obs_tile,
    obs_cell,
):
    state = level_filter(control, level_rate, False)
    state = x_filter(state, x_rate, False)
    increment = y_filter(state, y_rate, False)
    var_count, rows_here, cols_here, levels = increment.shape
    cell_count = rows_here * cols_here
    flat_state = increment.reshape(var_count, cell_count, levels)
    obs_here = innovation.shape[0]
    groups = lax.axis_size("gy")
    capacity = obs_here // 4
    window_count = groups * capacity
    target = obs_tile[:, 0]
    target_hot = (target[:, None] == lax.broadcasted_iota(jnp.int32, (obs_here, groups), 1)).astype(
        jnp.int32
    )
    rank_of = jnp.sum(jnp.cumsum(target_hot, axis=0) * target_hot, axis=1) - 1
    slot_of = target * capacity + rank_of
    placed = slot_of[:, None] == lax.broadcasted_iota(jnp.int32, (obs_here, window_count), 1)
    placing = placed.astype(jnp.float32)
    sent_cells = jnp.sum(jnp.where(placed, obs_cell[:, None] + 1, 0), axis=0).reshape(
        groups, capacity
    )
    landed = lax.all_to_all(sent_cells, "gy", split_axis=0, concat_axis=0, tiled=True).reshape(
        window_count
    )
    picking = (
        (landed - 1)[:, None] == lax.broadcasted_iota(jnp.int32, (window_count, cell_count), 1)
    ).astype(jnp.float32)
    state_profiles = jnp.einsum("sn,vnl->svl", picking, flat_state, precision=exact_result)
    window_radiances = jnp.einsum("fjz,jzt->ft", state_profiles, jacobian, precision=exact_result)
    returned = lax.all_to_all(
        window_radiances.reshape(groups, capacity, -1),
        "gy",
        split_axis=0,
        concat_axis=0,
        tiled=True,
    )
    channel_radiances = jnp.dot(placing, returned.reshape(window_count, -1), precision=exact_result)
    bias_values = jnp.dot(predictors, bias_coef, precision=exact_result)
    departures = innovation - channel_radiances - bias_values
    weighted_departures = departures * inv_var[None, :]
    slot_weights = jnp.dot(jnp.transpose(placing), weighted_departures, precision=exact_result)
    received_values = lax.all_to_all(
        slot_weights.reshape(groups, capacity, -1), "gy", split_axis=0, concat_axis=0, tiled=True
    )
    slot_grads = jnp.einsum(
        "yu,gru->ygr", received_values.reshape(window_count, -1), jacobian, precision=exact_result
    )
    column_gradients = jnp.einsum(
        "sn,svl->vnl", picking, slot_grads, precision=exact_result
    ).reshape(var_count, rows_here, cols_here, levels)
    state = y_filter(column_gradients, y_rate, True)
    state = x_filter(state, x_rate, True)
    obs_gradient = level_filter(state, level_rate, True)
    bias_terms = -jnp.dot(jnp.transpose(predictors), weighted_departures, precision=exact_result)
    cost_term = 0.5 * jnp.sum(departures * weighted_departures)
    bias_sum, cost_sum = lax.psum((bias_terms, cost_term), ("gx", "gy"))
    obs_total = obs_here * lax.axis_size("gx") * lax.axis_size("gy")
    return (obs_gradient, departures, bias_sum * obs_total ** (-0.5), cost_sum / obs_total)


def solution(mesh):
    return jax.shard_map(
        shards,
        mesh=mesh,
        in_specs=(
            P(None, "gy", "gx", None),
            P(),
            P(),
            P(),
            P(),
            P(("gx", "gy"), None),
            P(("gx", "gy"), None),
            P(),
            P(),
            P(("gx", "gy"), None),
            P(("gx", "gy")),
        ),
        out_specs=(P(None, "gy", "gx", None), P(("gx", "gy"), None), P(), P()),
        check_vma=False,
    )
```

profile of v0, /device:TPU:0, one launch (start us, length us, event | category | flops | bytes accessed | tf_op | source)
XLA Modules:
  0.0 285.3 jit_solution(2745913326229599230)
XLA Ops:
  0.7 0.8 subtract_log_fusion
  1.5 0.3 reduce_window_sum.35
  1.8 2.6 convolution_bitcast_fusion.5
  4.4 1.6 copy.120
  6.0 5.3 %all-to-all-start.1 = ((f32[4,32,16,128]{3,2,0,1:T(8,128)}), f32[4,32,16,128]{3,2,0,1:T(8,128)S(1)}, u32[]{:S(2)}, u32[]{:S(2)}) async-start(f32[4,32,16,128]{3,2,0,1:T(8,128)} %copy.120), calls=%async_computation.1 | async-start | bytes 2097152 | tf_op jit(solution)/shard_map/all_to_all | solution.py:26
  11.3 0.1 copy.123
  11.4 0.2 reduce-window.16
  11.6 0.1 reduce.1
  11.7 15.0 %all-to-all-done.1 = f32[4,32,16,128]{3,2,0,1:T(8,128)S(1)} async-done(((f32[4,32,16,128]{3,2,0,1:T(8,128)}), f32[4,32,16,128]{3,2,0,1:T(8,128)S(1)}, u32[]{:S(2)}, u32[]{:S(2)}) %all-to-all-start.1) | async-done | bytes 1048608 | tf_op jit(solution)/shard_map/all_to_all | solution.py:26
  26.7 0.1 copy.122
  26.8 1.8 convolution_bitcast_fusion.4
  28.6 0.6 copy.125
  29.3 17.8 %all_to_all.160 = f32[4,4,128,128]{3,1,0,2:T(4,128)S(1)} all-to-all(f32[4,4,128,128]{3,1,0,2:T(4,128)S(1)} %copy.125), channel_id=1, replica_groups=mesh['gx'=8,'gy'=4] {'gx'}, dimensions={2} | all-to-all | bytes 2097152 | tf_op jit(solution)/shard_map/all_to_all | solution.py:29
  47.0 0.3 copy.126
  47.4 0.1 copy.127
  47.5 1.3 copy.128
  48.8 5.0 %all-to-all-start.3 = ((f32[4,32,16,128]{3,1,0,2:T(8,128)}), f32[4,32,16,128]{3,1,0,2:T(8,128)S(1)}, u32[]{:S(2)}, u32[]{:S(2)}) async-start(f32[4,32,16,128]{3,1,0,2:T(8,128)} %copy.128), calls=%async_computation.3 | async-start | bytes 2097152 | tf_op jit(solution)/shard_map/all_to_all | solution.py:35
  53.8 0.1 copy.131
  53.9 0.2 reduce-window.17
  54.1 0.1 reduce.2
  54.3 0.2 reduce_window_sum.34
  54.5 0.2 select_reduce_fusion.1
  54.7 0.1 select_reduce_fusion
  54.8 0.7 all_to_all.114
  55.5 23.5 %all-to-all-done.3 = f32[4,32,16,128]{3,1,0,2:T(8,128)S(1)} async-done(((f32[4,32,16,128]{3,1,0,2:T(8,128)}), f32[4,32,16,128]{3,1,0,2:T(8,128)S(1)}, u32[]{:S(2)}, u32[]{:S(2)}) %all-to-all-start.3) | async-done | bytes 1048608 | tf_op jit(solution)/shard_map/all_to_all | solution.py:35
  79.0 3.2 %all-to-all-start = ((s32[4,1,32]{2,1,0:T(1,128)}), s32[4,1,32]{2,1,0:T(1,128)S(1)}, u32[]{:S(2)}, u32[]{:S(2)}) async-start(s32[4,1,32]{2,1,0:T(1,128)} %bitcast.3), calls=%async_computation | async-start | bytes 4096 | tf_op jit(solution)/shard_map/all_to_all | solution.py:90
  82.3 1.8 convolution_bitcast_fusion.3
  84.1 1.4 copy.133
  85.5 2.2 all-to-all-done
  87.7 3.5 %all-to-all-start.4 = ((f32[4,128,4,128]{3,2,0,1:T(4,128)}), f32[4,128,4,128]{3,2,0,1:T(4,128)S(1)}, u32[]{:S(2)}, u32[]{:S(2)}) async-start(f32[4,128,4,128]{3,2,0,1:T(4,128)} %copy.133), calls=%async_computation.4 | async-start | bytes 2097152 | tf_op jit(solution)/shard_map/all_to_all | solution.py:38
  91.3 24.0 %all-to-all-done.4 = f32[4,128,4,128]{3,2,0,1:T(4,128)S(1)} async-done(((f32[4,128,4,128]{3,2,0,1:T(4,128)}), f32[4,128,4,128]{3,2,0,1:T(4,128)S(1)}, u32[]{:S(2)}, u32[]{:S(2)}) %all-to-all-start.4) | async-done | bytes 1048608 | tf_op jit(solution)/shard_map/all_to_all | solution.py:38
  115.3 0.3 copy.134
  115.6 0.7 copy.135
  116.3 0.5 fusion.12
  116.9 2.1 fusion.60
  119.1 3.6 %all-to-all-start.5 = ((f32[4,32,616]{2,1,0:T(8,128)}), f32[4,32,616]{2,1,0:T(8,128)S(1)}, u32[]{:S(2)}, u32[]{:S(2)}) async-start(f32[4,32,616]{2,1,0:T(8,128)} %bitcast.31), calls=%async_computation.5 | async-start | bytes 655360 | tf_op jit(solution)/shard_map/all_to_all | solution.py:98
  122.7 0.7 fusion.61
  123.5 8.9 %all-to-all-done.5 = f32[4,32,616]{2,1,0:T(8,128)S(1)} async-done(((f32[4,32,616]{2,1,0:T(8,128)}), f32[4,32,616]{2,1,0:T(8,128)S(1)}, u32[]{:S(2)}, u32[]{:S(2)}) %all-to-all-start.5) | async-done | bytes 315424 | tf_op jit(solution)/shard_map/all_to_all | solution.py:98
  132.3 1.1 fusion.6
  133.4 0.7 copy-done.1
  134.1 0.5 fusion.4
  134.6 11.8 %all_to_all.161 = f32[4,32,616]{2,1,0:T(8,128)S(1)} all-to-all(f32[4,32,616]{2,1,0:T(8,128)S(1)} %bitcast.125), channel_id=1, replica_groups=mesh['gx'=8,'gy'=4] {'gy'}, dimensions={0} | all-to-all | bytes 630784 | tf_op jit(solution)/shard_map/all_to_all | solution.py:110
  146.4 2.3 fusion.62
  148.7 0.7 convolution_bitcast_fusion.2
  149.3 0.3 copy.140
  149.7 0.3 copy.141
  150.0 27.4 %all_to_all.162 = f32[4,32,16,128]{3,1,0,2:T(8,128)S(1)} all-to-all(f32[4,32,16,128]{3,1,0,2:T(8,128)S(1)} %copy.141), channel_id=1, replica_groups=mesh['gx'=8,'gy'=4] {'gy'}, dimensions={2} | all-to-all | bytes 2097152 | tf_op jit(solution)/shard_map/all_to_all | solution.py:35
  177.5 1.8 convolution_bitcast_fusion.1
  179.3 0.6 copy.145
  179.9 27.6 %all_to_all.163 = f32[4,128,4,128]{3,2,0,1:T(4,128)S(1)} all-to-all(f32[4,128,4,128]{3,2,0,1:T(4,128)S(1)} %copy.145), channel_id=1, replica_groups=mesh['gx'=8,'gy'=4] {'gy'}, dimensions={1} | all-to-all | bytes 2097152 | tf_op jit(solution)/shard_map/all_to_all | solution.py:38
  207.6 0.3 copy.146
  207.9 0.1 copy.147
  208.0 0.6 copy.148
  208.6 17.8 %all_to_all.164 = f32[4,32,16,128]{3,2,0,1:T(8,128)S(1)} all-to-all(f32[4,32,16,128]{3,2,0,1:T(8,128)S(1)} %copy.148), channel_id=1, replica_groups=mesh['gx'=8,'gy'=4] {'gx'}, dimensions={1} | all-to-all | bytes 2097152 | tf_op jit(solution)/shard_map/all_to_all | solution.py:26
  226.4 0.1 copy.150
  226.5 1.8 convolution_bitcast_fusion
  228.4 1.4 copy.152
  229.7 3.7 %all-to-all-start.10 = ((f32[4,4,128,128]{3,1,0,2:T(4,128)}), f32[4,4,128,128]{3,1,0,2:T(4,128)S(1)}, u32[]{:S(2)}, u32[]{:S(2)}) async-start(f32[4,4,128,128]{3,1,0,2:T(4,128)} %copy.152), calls=%async_computation.10 | async-start | bytes 2097152 | tf_op jit(solution)/shard_map/all_to_all | solution.py:29
  234.1 0.5 fusion.1
  234.6 45.7 %all-reduce = (f32[8,616]{1,0:T(8,128)S(1)}, f32[]{:T(128)}) all-reduce(f32[8,616]{1,0:T(8,128)S(1)} %fusion.1, f32[]{:T(128)S(6)} %mul_shard_map.3), channel_id=1, replica_groups=mesh['gx'=8,'gy'=4] {'gx','gy'}, use_global_device_ids=true, to_apply=%region_6.7 | all-reduce | flops 4929 | bytes 39432 | tf_op jit(solution)/shard_map/psum | solution.py:124
  281.0 0.6 broadcast_multiply_fusion
  281.6 0.3 copy.153
  281.9 0.1 copy.154
  282.1 2.1 fusion.7
  (32 shorter events, 0.5 us)
Async XLA Ops:
  0.6 116.3 %copy-start = (f32[4,128,616]{1,2,0:T(8,128)S(1)}, f32[4,128,616]{1,2,0:T(8,128)}, u32[]{:S(2)}) copy-start(f32[4,128,616]{1,2,0:T(8,128)} %param.15) | copy-start | bytes 3784708
  6.0 5.3 %copy-start.8 = (f32[128]{0:T(128)S(1)}, f32[128]{0:T(128)}, u32[]{:S(2)}) copy-start(f32[128]{0:T(128)} %param.13) | copy-start | bytes 1540
  6.0 20.7 %all-to-all-start.1 = ((f32[4,32,16,128]{3,2,0,1:T(8,128)}), f32[4,32,16,128]{3,2,0,1:T(8,128)S(1)}, u32[]{:S(2)}, u32[]{:S(2)}) async-start(f32[4,32,16,128]{3,2,0,1:T(8,128)} %copy.120), calls=%async_computation.1 | async-start | bytes 2097152 | tf_op jit(solution)/shard_map/all_to_all | solution.py:26
  48.8 5.0 %copy-start.9 = (f32[128]{0:T(128)S(1)}, f32[128]{0:T(128)}, u32[]{:S(2)}) copy-start(f32[128]{0:T(128)} %param.14) | copy-start | bytes 1540
  48.8 5.4 %copy-start.7 = (s32[128,1]{0,1:T(1,128)S(1)}, s32[128,1]{0,1:T(1,128)}, u32[]{:S(2)}) copy-start(s32[128,1]{0,1:T(1,128)} %param.20) | copy-start | bytes 1540
  48.8 5.9 %copy-start.10 = (s32[128]{0:T(128)S(1)}, s32[128]{0:T(128)}, u32[]{:S(2)}) copy-start(s32[128]{0:T(128)} %param.21) | copy-start | bytes 1540
  48.8 30.2 %all-to-all-start.3 = ((f32[4,32,16,128]{3,1,0,2:T(8,128)}), f32[4,32,16,128]{3,1,0,2:T(8,128)S(1)}, u32[]{:S(2)}, u32[]{:S(2)}) async-start(f32[4,32,16,128]{3,1,0,2:T(8,128)} %copy.128), calls=%async_computation.3 | async-start | bytes 2097152 | tf_op jit(solution)/shard_map/all_to_all | solution.py:35
  79.0 8.7 %all-to-all-start = ((s32[4,1,32]{2,1,0:T(1,128)}), s32[4,1,32]{2,1,0:T(1,128)S(1)}, u32[]{:S(2)}, u32[]{:S(2)}) async-start(s32[4,1,32]{2,1,0:T(1,128)} %bitcast.3), calls=%async_computation | async-start | bytes 4096 | tf_op jit(solution)/shard_map/all_to_all | solution.py:90
  87.7 27.6 %all-to-all-start.4 = ((f32[4,128,4,128]{3,2,0,1:T(4,128)}), f32[4,128,4,128]{3,2,0,1:T(4,128)S(1)}, u32[]{:S(2)}, u32[]{:S(2)}) async-start(f32[4,128,4,128]{3,2,0,1:T(4,128)} %copy.133), calls=%async_computation.4 | async-start | bytes 2097152 | tf_op jit(solution)/shard_map/all_to_all | solution.py:38
  116.9 5.8 %copy-start.5 = (f32[8,616]{1,0:T(8,128)S(1)}, f32[8,616]{1,0:T(8,128)}, u32[]{:S(2)}) copy-start(f32[8,616]{1,0:T(8,128)} %param.18) | copy-start | bytes 59140
  116.9 5.8 %copy-start.6 = (f32[128,8]{0,1:T(8,128)S(1)}, f32[128,8]{0,1:T(8,128)}, u32[]{:S(2)}) copy-start(f32[128,8]{0,1:T(8,128)} %param.17) | copy-start | bytes 12292
  116.9 15.4 %copy-start.3 = (f32[128,616]{0,1:T(8,128)S(1)}, f32[128,616]{0,1:T(8,128)}, u32[]{:S(2)}) copy-start(f32[128,616]{0,1:T(8,128)} %param.16) | copy-start | bytes 946180
  116.9 15.4 %copy-start.4 = (f32[616]{0:T(1024)S(1)}, f32[616]{0:T(1024)}, u32[]{:S(2)}) copy-start(f32[616]{0:T(1024)} %param.19) | copy-start | bytes 7396
  119.1 13.3 %all-to-all-start.5 = ((f32[4,32,616]{2,1,0:T(8,128)}), f32[4,32,616]{2,1,0:T(8,128)S(1)}, u32[]{:S(2)}, u32[]{:S(2)}) async-start(f32[4,32,616]{2,1,0:T(8,128)} %bitcast.31), calls=%async_computation.5 | async-start | bytes 655360 | tf_op jit(solution)/shard_map/all_to_all | solution.py:98
  133.4 0.7 copy-start.1
  229.7 4.3 %copy-start.2 = (f32[128,616]{0,1:T(8,128)S(1)}, f32[128,616]{0,1:T(8,128)}, u32[]{:S(2)}) copy-start(f32[128,616]{0,1:T(8,128)} %copy-done.1) | copy-start | bytes 946180
  229.7 51.9 %all-to-all-start.10 = ((f32[4,4,128,128]{3,1,0,2:T(4,128)}), f32[4,4,128,128]{3,1,0,2:T(4,128)S(1)}, u32[]{:S(2)}, u32[]{:S(2)}) async-start(f32[4,4,128,128]{3,1,0,2:T(4,128)} %copy.152), calls=%async_computation.10 | async-start | bytes 2097152 | tf_op jit(solution)/shard_map/all_to_all | solution.py:29
where the time goes:
time: 286 us; the launch traced here: 285 us
  blocking collectives  148 us (52%)
  waiting for transfers between devices  73.5 us (26%)
  starting transfers between devices  24.4 us (9%)
  matrix products  20.4 us (7%)
  local copies, waits for them, and re-layouts  12.7 us (4%)
  between operations  3.43 us (1%)
  other arithmetic  2.86 us (1%)
    psum x1, blocking collectives, shards(): bias_sum, cost_sum = lax.psum((bias_terms, cost_term), ('gx', 'gy'))  45.7 us
    all_to_all x1, blocking collectives, y_transposed(): lax.all_to_all(filtered, 'gy', split_axis=1, concat_axis=2, tiled=True)  27.6 us
    all_to_all x1, blocking collectives, y_transposed(): lax.all_to_all(state, 'gy', split_axis=2, concat_axis=1, tiled=True)  27.4 us
    all_to_all x1, waiting for transfers between devices, y_transposed(): lax.all_to_all(filtered, 'gy', split_axis=1, concat_axis=2, tiled=True)  24 us
    all_to_all x1, waiting for transfers between devices, y_transposed(): lax.all_to_all(state, 'gy', split_axis=2, concat_axis=1, tiled=True)  23.5 us
    all_to_all x1, blocking collectives, x_transposed(): lax.all_to_all(filtered, 'gx', split_axis=2, concat_axis=1, tiled=True)  17.8 us
    all_to_all x1, blocking collectives, x_transposed(): lax.all_to_all(state, 'gx', split_axis=1, concat_axis=2, tiled=True)  17.8 us
    all_to_all x1, waiting for transfers between devices, x_transposed(): lax.all_to_all(state, 'gx', split_axis=1, concat_axis=2, tiled=True)  15 us
  transfers between devices with their start and end apart: 6, of which 5 were waited for; matrix products, arithmetic and copies ran while one was open for 2% of the time, Pallas kernels for 0%

commit v1 on v0

v1 whole, which is shorter than its diff:
```python
import functools

import jax
import jax.numpy as jnp
from jax import lax
from jax.experimental import pallas as pl
from jax.experimental.pallas import tpu as pltpu
from jax.sharding import PartitionSpec as P

MESH = pl.DeviceIdType.MESH
F32 = jnp.float32
BF16 = jnp.bfloat16
CUT = -1e30

X_ENDS, X_CORNER, X_CARRY, X_BACK_CORNER, X_BIAS = range(5)
Y_CELLS, Y_ENDS, Y_CORNER, Y_PROF, Y_GRAD, Y_BIAS, Y_CARRY, Y_BACK_CORNER = range(8)


def iota(shape, axis):
    return lax.broadcasted_iota(jnp.int32, shape, axis)


def split(value):
    high = value.astype(BF16)
    return high, (value - high.astype(F32)).astype(BF16)


def mm(left, right, dims):
    return lax.dot_general(left, right, (dims, ((), ())), preferred_element_type=F32)


def mm3(left, right, dims=((1,), (0,))):
    (lh, ll), (rh, rl) = left, right
    return mm(lh, rh, dims) + (mm(lh, rl, dims) + mm(ll, rh, dims))


def to_col(row):
    size = row.shape[1]
    diag = iota((size, size), 0) == iota((size, size), 1)
    return jnp.sum(jnp.where(diag, row, 0.0), axis=1, keepdims=True)


def logs(rates):
    decays = 1.0 - rates
    return jnp.log(decays), 0.5 * jnp.log(1.0 - decays * decays)


def sums_both(row, start):
    size = row.shape[1]
    at0, at1 = iota((size, size), 0), iota((size, size), 1)
    as_row = jnp.sum(jnp.where((at0 <= at1) & (at0 >= start), to_col(row), 0.0), axis=0, keepdims=True)
    as_col = jnp.sum(jnp.where((at1 <= at0) & (at1 >= start), row, 0.0), axis=1, keepdims=True)
    return as_row, as_col


def between(row, me, count, width):
    size = row.shape[1]
    other, lane = iota((count, size), 0), iota((count, size), 1)
    after = (lane >= (other + 1) * width) & (lane < me * width)
    before = (lane >= (me + 1) * width) & (lane < other * width)
    fwd = jnp.exp(jnp.sum(jnp.where(after, row, 0.0), axis=1, keepdims=True))
    bwd = jnp.exp(jnp.sum(jnp.where(before, row, 0.0), axis=1, keepdims=True))
    return fwd, bwd


def kernel(
    nx, ny, control, level_rate, x_rate, y_rate, jacobian, innovation, pred_t, bias_coef, inv_var, tile_row,
    cell_row, grad_out, dep_out, bias_out, cost_out,
    state, jac, innov, state_h, state_l, jf_h, jf_l, decay_x, decay_y, carry,
    x_send, x_recv, y_send, y_recv, c_send, c_recv, c2_send, c2_recv,
    cells_send, cells_recv, prof_send, prof_recv, gsl_send, gsl_recv,
    bx_send, bx_recv, by_send, by_recv, bc_send, bc_recv, bc2_send, bc2_recv,
    b1_recv, b2_recv, b1_send, b2_send, local_sem, sx_sem, rx_sem, sy_sem, ry_sem,
):
    gx, gy = lax.axis_index("gx"), lax.axis_index("gy")
    variables, rows, cols, levels = control.shape
    cells = rows * cols
    channels = innovation.shape[1]
    obs = innovation.shape[0]
    cap = prof_send.shape[1]
    slots = ny * cap
    width = variables * levels
    ends = rows + cols + 8

    loads = [
        pltpu.make_async_copy(control, state, local_sem.at[0]),
        pltpu.make_async_copy(jacobian, jac, local_sem.at[1]),
        pltpu.make_async_copy(innovation, innov, local_sem.at[2]),
    ]
    for load in loads:
        load.start()

    barrier = pltpu.get_barrier_semaphore()

    def each(count, me, act, when):
        def body(t, _):
            @pl.when(when(t, me))
            def _():
                act(t)
            return 0
        lax.fori_loop(0, count, body, 0)

    other = lambda t, me: t != me
    later = lambda t, me: t > me
    earlier = lambda t, me: t < me

    def greet_x(t):
        pl.semaphore_signal(barrier, inc=1, device_id=(t, gy), device_id_type=MESH)

    def greet_y(t):
        pl.semaphore_signal(barrier, inc=1, device_id=(gx, t), device_id_type=MESH)

    each(nx, gx, greet_x, other)
    each(ny, gy, greet_y, other)

    def x_copy(row, src, dst, target, slot):
        return pltpu.make_async_remote_copy(
            src_ref=src, dst_ref=dst.at[slot], send_sem=sx_sem.at[row, target], recv_sem=rx_sem.at[row, slot],
            device_id=(target, gy), device_id_type=MESH)

    def y_copy(row, src, dst, target, slot):
        return pltpu.make_async_remote_copy(
            src_ref=src, dst_ref=dst.at[slot], send_sem=sy_sem.at[row, target], recv_sem=ry_sem.at[row, slot],
            device_id=(gx, target), device_id_type=MESH)

    tile_r = tile_row[...].astype(F32)
    cell_r = cell_row[...].astype(F32)
    tile_c = to_col(tile_r)
    at0, at1 = iota((obs, obs), 0), iota((obs, obs), 1)
    same = tile_c == tile_r
    rank_c = jnp.sum(jnp.where(same & (at1 < at0), 1.0, 0.0), axis=1, keepdims=True)
    rank_r = jnp.sum(jnp.where(same & (at0 < at1), 1.0, 0.0), axis=0, keepdims=True)
    slot_c = (tile_c * cap + rank_c).astype(jnp.int32)
    slot_r = (tile_r * cap + rank_r).astype(jnp.int32)
    placing = jnp.where(slot_c == iota((obs, slots), 1), 1.0, 0.0).astype(BF16)
    placed_t = slot_r == iota((slots, obs), 0)
    placing_t = jnp.where(placed_t, 1.0, 0.0).astype(BF16)
    sent = jnp.sum(jnp.where(placed_t, cell_r + 1.0, 0.0), axis=1, keepdims=True)
    cells_send[...] = jnp.broadcast_to(sent, (slots, 128)).reshape(ny, cap, 128)
    cells_recv[gy] = cells_send[gy]

    x_log, x_scale = logs(x_rate[...])
    y_log, y_scale = logs(y_rate[...])
    fwd, bwd = between(x_log, gx, nx, cols)
    decay_x[0] = jnp.broadcast_to(fwd, (nx, 128))
    decay_x[1] = jnp.broadcast_to(bwd, (nx, 128))
    fwd, bwd = between(y_log, gy, ny, rows)
    decay_y[0] = jnp.broadcast_to(fwd, (ny, 128))
    decay_y[1] = jnp.broadcast_to(bwd, (ny, 128))
    sx_r, sx_c = sums_both(x_log, gx * cols)
    sy_r, sy_c = sums_both(y_log, gy * rows)
    qx_c = sx_c - to_col(x_scale)
    qy_c = sy_c - to_col(y_scale)

    def total(row, start, size):
        lane = iota(row.shape, 1)
        return jnp.sum(jnp.where((lane >= start) & (lane < start + size), row, 0.0), axis=1, keepdims=True)

    t_x, t_y = total(x_log, gx * cols, cols), total(y_log, gy * rows, rows)

    n = iota((1, cells), 1)
    y_n = n // cols
    x_n = n - y_n * cols

    def pick_rows(col, at):
        return jnp.sum(jnp.where(iota((col.shape[0], at.shape[1]), 0) == at, col, 0.0), axis=0, keepdims=True)

    qx_n = pick_rows(qx_c, x_n + gx * cols)
    qy_n = pick_rows(qy_c, y_n + gy * rows)
    e = iota((ends, 1), 0)
    on_x = (e < rows) & (e == y_n)
    on_y = (e >= rows) & (e - rows == x_n) & (e < rows + cols)
    to_x, to_y = t_x - qx_n, t_y - qy_n
    e_log = jnp.where(on_x, to_x, jnp.where(on_y, to_y, jnp.where(e == rows + cols, to_x + to_y, CUT)))
    e_parts = split(jnp.exp(e_log))

    pl.semaphore_wait(barrier, nx + ny - 2)
    each(ny, gy, lambda t: y_copy(Y_CELLS, cells_send.at[t], cells_recv, t, gy).start(), other)

    loads[0].wait()
    for v in range(variables):
        high, low = split(state[v].reshape(cells, levels))
        state_h[:, v * levels:(v + 1) * levels] = high
        state_l[:, v * levels:(v + 1) * levels] = low
    field = (state_h[...], state_l[...])
    tails = mm3(e_parts, field)
    x_send[...] = tails[0:rows]
    y_send[...] = tails[rows:rows + cols]
    c_send[...] = tails[rows + cols:rows + cols + 1]
    each(nx, gx, lambda t: x_copy(X_CORNER, c_send, c_recv, t, gx).start(), later)
    each(nx, gx, lambda t: x_copy(X_ENDS, x_send, x_recv, t, gx).start(), later)
    each(ny, gy, lambda t: y_copy(Y_ENDS, y_send, y_recv, t, gy).start(), later)

    carry[...] = jnp.zeros_like(carry)

    def widen(ref, side, t):
        row = ref[side, pl.ds(t, 1), :]
        return jnp.concatenate([row] * (width // 128), axis=1)

    each(ny, gy, lambda t: y_copy(Y_CELLS, cells_send.at[t], cells_recv, t, t).wait_recv(), other)
    landed = cells_recv[...].reshape(slots, 128)[:, 0:1] - 1.0
    y_s = jnp.floor((landed + 0.5) * (1.0 / cols))
    x_s = (landed - y_s * cols).astype(jnp.int32)
    y_s = jnp.where(landed < 0.0, -5.0, y_s).astype(jnp.int32)

    def pick_cols(row, at):
        return jnp.sum(jnp.where(iota((at.shape[0], row.shape[1]), 1) == at, row, 0.0), axis=1, keepdims=True)

    sx_s = pick_cols(sx_r, x_s + gx * cols)
    sy_s = pick_cols(sy_r, jnp.where(y_s < 0, -1, y_s + gy * rows))
    reach = (y_n <= y_s) & (x_n <= x_s)
    w_cells = split(jnp.exp(jnp.where(reach, (sy_s + sx_s) - (qy_n + qx_n), CUT)))
    c = iota((1, ends), 1)
    qy_e = pick_rows(qy_c, jnp.where(c < rows, c + gy * rows, -1))
    qx_e = pick_rows(qx_c, jnp.where((c >= rows) & (c < rows + cols), c - rows + gx * cols, -1))
    y_e = jnp.where(c < rows, c, -1)
    x_e = jnp.where((c >= rows) & (c < rows + cols), c - rows, -1)
    reach_e = (y_e <= y_s) & (x_e <= x_s) & (y_s >= 0) & (c <= rows + cols)
    w_carry = split(jnp.exp(jnp.where(reach_e, (sy_s + sx_s) - (qy_e + qx_e), CUT)))

    def add_corner(t):
        x_copy(X_CORNER, c_send, c_recv, t, t).wait_recv()
        carry[rows + cols:rows + cols + 1, :] += widen(decay_x, 0, t) * c_recv[t]

    each(nx, gx, add_corner, earlier)
    c2_send[...] = carry[rows + cols:rows + cols + 1, :]
    each(ny, gy, lambda t: y_copy(Y_CORNER, c2_send, c2_recv, t, gy).start(), later)
    carry[rows + cols:rows + cols + 1, :] = jnp.zeros((1, width), F32)

    prof = mm3(w_cells, field)

    loads[1].wait()
    l_log, l_scale = logs(level_rate[...])
    m0, m1 = iota((levels, levels), 0), iota((levels, levels), 1)
    for v in range(variables):
        s_r, s_c = sums_both(l_log[v:v + 1, :], 0)
        q_c = s_c - to_col(l_scale[v:v + 1, :])
        f_t = split(jnp.exp(jnp.where(m0 <= m1, s_r - q_c, CUT)))
        high, low = split(mm3(f_t, split(jac[v])))
        jf_h[v * levels:(v + 1) * levels, :] = high
        jf_l[v * levels:(v + 1) * levels, :] = low

    loads[2].wait()
    pred = split(pred_t[...])
    base = innov[...] - mm3(pred, split(bias_coef[...]), ((0,), (0,)))

    def add_x(t):
        x_copy(X_ENDS, x_send, x_recv, t, t).wait_recv()
        carry[0:rows, :] += widen(decay_x, 0, t) * x_recv[t]

    def add_y(t):
        y_copy(Y_ENDS, y_send, y_recv, t, t).wait_recv()
        carry[rows:rows + cols, :] += widen(decay_y, 0, t) * y_recv[t]

    def add_c2(t):
        y_copy(Y_CORNER, c2_send, c2_recv, t, t).wait_recv()
        carry[rows + cols:rows + cols + 1, :] += widen(decay_y, 0, t) * c2_recv[t]

    each(ny, gy, add_y, earlier)
    each(nx, gx, add_x, earlier)
    each(ny, gy, add_c2, earlier)
    prof = prof + mm3(w_carry, split(carry[...]))
    prof_send[...] = prof.reshape(ny, cap, width)
    each(ny, gy, lambda t: y_copy(Y_PROF, prof_send.at[t], prof_recv, t, gy).start(), other)
    prof_recv[gy] = prof_send[gy]
    each(ny, gy, lambda t: y_copy(Y_PROF, prof_send.at[t], prof_recv, t, t).wait_recv(), other)

    got_h, got_l = split(prof_recv[...].reshape(slots, width))
    nn = ((1,), (0,))
    own = (mm(placing, got_h, nn).astype(BF16), mm(placing, got_l, nn).astype(BF16))
    jf = (jf_h[...], jf_l[...])
    departures = base - mm3(own, jf)
    dep_out[...] = departures
    weighted = departures * inv_var[...]
    w_parts = split(weighted)
    g_h, g_l = split(mm3(w_parts, jf, ((1,), (1,))))
    gsl_send[...] = (mm(placing_t, g_h, nn) + mm(placing_t, g_l, nn)).reshape(ny, cap, width)
    each(ny, gy, lambda t: y_copy(Y_GRAD, gsl_send.at[t], gsl_recv, t, gy).start(), other)
    gsl_recv[gy] = gsl_send[gy]

    b1_send[:, 0:channels] = -mm3(pred, w_parts)
    cost = jnp.sum(jnp.sum(departures * weighted, axis=1, keepdims=True), axis=0, keepdims=True)
    b1_send[:, channels:] = jnp.broadcast_to(0.5 * cost, (b1_send.shape[0], b1_send.shape[1] - channels))
    each(ny, gy, lambda t: y_copy(Y_BIAS, b1_send, b1_recv, t, gy).start(), other)
    b1_recv[gy] = b1_send[...]

    each(ny, gy, lambda t: y_copy(Y_GRAD, gsl_send.at[t], gsl_recv, t, t).wait_recv(), other)
    grads = split(gsl_recv[...].reshape(slots, width))
    tn = ((0,), (0,))
    out = mm3(w_carry, grads, tn)
    bx_send[...] = out[0:rows]
    by_send[...] = out[rows:rows + cols]
    bc_send[...] = out[rows + cols:rows + cols + 1]
    each(nx, gx, lambda t: x_copy(X_BACK_CORNER, bc_send, bc_recv, t, gx).start(), earlier)
    each(nx, gx, lambda t: x_copy(X_CARRY, bx_send, bx_recv, t, gx).start(), earlier)
    each(ny, gy, lambda t: y_copy(Y_CARRY, by_send, by_recv, t, gy).start(), earlier)

    each(ny, gy, lambda t: y_copy(Y_BIAS, b1_send, b1_recv, t, t).wait_recv(), other)
    b2_send[...] = jnp.sum(b1_recv[...], axis=0)
    each(nx, gx, lambda t: x_copy(X_BIAS, b2_send, b2_recv, t, gx).start(), other)
    b2_recv[gx] = b2_send[...]

    carry[...] = jnp.zeros_like(carry)

    def back_corner(t):
        x_copy(X_BACK_CORNER, bc_send, bc_recv, t, t).wait_recv()
        carry[rows + cols:rows + cols + 1, :] += widen(decay_x, 1, t) * bc_recv[t]

    each(nx, gx, back_corner, later)
    bc2_send[...] = carry[rows + cols:rows + cols + 1, :]
    each(ny, gy, lambda t: y_copy(Y_BACK_CORNER, bc2_send, bc2_recv, t, gy).start(), earlier)
    carry[rows + cols:rows + cols + 1, :] = jnp.zeros((1, width), F32)

    here = mm3(w_cells, grads, tn)

    def back_x(t):
        x_copy(X_CARRY, bx_send, bx_recv, t, t).wait_recv()
        carry[0:rows, :] += widen(decay_x, 1, t) * bx_recv[t]

    def back_y(t):
        y_copy(Y_CARRY, by_send, by_recv, t, t).wait_recv()
        carry[rows:rows + cols, :] += widen(decay_y, 1, t) * by_recv[t]

    def back_c2(t):
        y_copy(Y_BACK_CORNER, bc2_send, bc2_recv, t, t).wait_recv()
        carry[rows + cols:rows + cols + 1, :] += widen(decay_y, 1, t) * bc2_recv[t]

    each(ny, gy, back_y, later)
    each(nx, gx, back_x, later)
    each(ny, gy, back_c2, later)
    here = here + mm3(e_parts, split(carry[...]), tn)
    for v in range(variables):
        grad_out[v] = here[:, v * levels:(v + 1) * levels].reshape(rows, cols, levels)

    each(nx, gx, lambda t: x_copy(X_BIAS, b2_send, b2_recv, t, t).wait_recv(), other)
    summed = jnp.sum(b2_recv[...], axis=0)
    obs_total = obs * nx * ny
    bias_out[...] = summed[:, 0:channels] * obs_total ** -0.5
    cost_out[...] = summed[0:1, channels:channels + 1] * (1.0 / obs_total)

    each(ny, gy, lambda t: y_copy(Y_CELLS, cells_send.at[t], cells_recv, t, gy).wait_send(), other)
    each(ny, gy, lambda t: y_copy(Y_PROF, prof_send.at[t], prof_recv, t, gy).wait_send(), other)
    each(ny, gy, lambda t: y_copy(Y_GRAD, gsl_send.at[t], gsl_recv, t, gy).wait_send(), other)
    each(ny, gy, lambda t: y_copy(Y_BIAS, b1_send, b1_recv, t, gy).wait_send(), other)
    each(nx, gx, lambda t: x_copy(X_BIAS, b2_send, b2_recv, t, gx).wait_send(), other)

    def forward_x(t):
        x_copy(X_CORNER, c_send, c_recv, t, gx).wait_send()
        x_copy(X_ENDS, x_send, x_recv, t, gx).wait_send()

    def forward_y(t):
        y_copy(Y_ENDS, y_send, y_recv, t, gy).wait_send()
        y_copy(Y_CORNER, c2_send, c2_recv, t, gy).wait_send()

    def backward_x(t):
        x_copy(X_BACK_CORNER, bc_send, bc_recv, t, gx).wait_send()
        x_copy(X_CARRY, bx_send, bx_recv, t, gx).wait_send()

    def backward_y(t):
        y_copy(Y_CARRY, by_send, by_recv, t, gy).wait_send()
        y_copy(Y_BACK_CORNER, bc2_send, bc2_recv, t, gy).wait_send()

    each(nx, gx, forward_x, later)
    each(ny, gy, forward_y, later)
    each(nx, gx, backward_x, earlier)
    each(ny, gy, backward_y, earlier)


def shards(nx, ny, control, level_rate, x_rate, y_rate, jacobian, innovation, predictors, bias_coef, inv_var,
           obs_tile, obs_cell):
    variables, rows, cols, levels = control.shape
    obs, channels = innovation.shape
    cells, width = rows * cols, variables * levels
    cap = obs // 4
    kinds = predictors.shape[1]
    wide = (channels // 128 + 1) * 128
    ends = rows + cols + 8
    vmem = pl.BlockSpec(memory_space=pltpu.VMEM)
    anyw = pl.BlockSpec(memory_space=pl.ANY)
    both = lambda count, *shape: [pltpu.VMEM(shape, F32), pltpu.VMEM((count,) + shape, F32)]
    slotted = lambda *shape: [pltpu.VMEM((ny, cap) + shape, F32)] * 2
    grad, dep, bias, cost = pl.pallas_call(
        functools.partial(kernel, nx, ny),
        out_shape=(
            jax.ShapeDtypeStruct(control.shape, F32),
            jax.ShapeDtypeStruct(innovation.shape, F32),
            jax.ShapeDtypeStruct((kinds, channels), F32),
            jax.ShapeDtypeStruct((1, 1), F32),
        ),
        in_specs=[anyw, vmem, vmem, vmem, anyw, anyw, vmem, vmem, vmem, vmem, vmem],
        out_specs=(vmem, vmem, vmem, vmem),
        scratch_shapes=[
            pltpu.VMEM(control.shape, F32),
            pltpu.VMEM(jacobian.shape, F32),
            pltpu.VMEM(innovation.shape, F32),
            pltpu.VMEM((cells, width), BF16),
            pltpu.VMEM((cells, width), BF16),
            pltpu.VMEM((width, channels), BF16),
            pltpu.VMEM((width, channels), BF16),
            pltpu.VMEM((2, nx, 128), F32),
            pltpu.VMEM((2, ny, 128), F32),
            pltpu.VMEM((ends, width), F32),
            *both(nx, rows, width), *both(ny, cols, width), *both(nx, 1, width), *both(ny, 1, width),
            *slotted(128), *slotted(width), *slotted(width),
            *both(nx, rows, width), *both(ny, cols, width), *both(nx, 1, width), *both(ny, 1, width),
            pltpu.VMEM((ny, kinds, wide), F32), pltpu.VMEM((nx, kinds, wide), F32),
            pltpu.VMEM((kinds, wide), F32), pltpu.VMEM((kinds, wide), F32),
            pltpu.SemaphoreType.DMA((3,)),
            pltpu.SemaphoreType.DMA((5, nx)), pltpu.SemaphoreType.DMA((5, nx)),
            pltpu.SemaphoreType.DMA((8, ny)), pltpu.SemaphoreType.DMA((8, ny)),
        ],
        compiler_params=pltpu.CompilerParams(
            collective_id=0, has_side_effects=True, vmem_limit_bytes=60 * 1024 * 1024),
    )(control, level_rate, x_rate.reshape(1, -1), y_rate.reshape(1, -1), jacobian, innovation, predictors.T,
      bias_coef, inv_var.reshape(1, -1), obs_tile.reshape(1, -1), obs_cell.reshape(1, -1))
    return grad, dep, bias, cost[0, 0]


def solution(mesh):
    nx, ny = mesh.shape["gx"], mesh.shape["gy"]
    return jax.shard_map(
        functools.partial(shards, nx, ny),
        mesh=mesh,
        in_specs=(
            P(None, "gy", "gx", None),
            P(),
            P(),
            P(),
            P(),
            P(("gx", "gy"), None),
            P(("gx", "gy"), None),
            P(),
            P(),
            P(("gx", "gy"), None),
            P(("gx", "gy")),
        ),
        out_specs=(P(None, "gy", "gx", None), P(("gx", "gy"), None), P(), P()),
        check_vma=False,
    )
```

time: 286 us -> 57.1 us (0.20)
  blocking collectives: 148 us -> 0 us
  waiting for transfers between devices: 73.5 us -> 0 us
  Pallas kernels: 0 us -> 43.6 us
  starting transfers between devices: 24.4 us -> 0 us
  matrix products: 20.4 us -> 0 us
  other arithmetic: 2.86 us -> 0 us
    all_to_all x5 -> x0, blocking collectives: 102 us -> none  [the longest x1 27.6 us: y_transposed(): lax.all_to_all(filtered, 'gy', split_axis=1, concat_axis=2, tiled=True)]
    all_to_all x6 -> x0, waiting for transfers between devices: 73.5 us -> none  [the longest x1 24 us: y_transposed(): lax.all_to_all(filtered, 'gy', split_axis=1, concat_axis=2, tiled=True)]
    psum x1 -> x0, blocking collectives: 45.7 us -> none  [shards(): bias_sum, cost_sum = lax.psum((bias_terms, cost_term), ('gx', 'gy'))]
    pallas_call x0 -> x1, Pallas kernels: none -> 43.6 us  [shards(): pl.pallas_call(functools.partial(kernel, nx, ny), out_shape=(jax.ShapeDty...]
    all_to_all x6 -> x0, starting transfers between devices: 24.4 us -> none  [the longest x1 5.33 us: x_transposed(): lax.all_to_all(state, 'gx', split_axis=1, concat_axis=2, tiled=True)]
    dot_general x14 -> x0, matrix products: 20.4 us -> none  [the longest x2 4.71 us: level_filter(): return jnp.einsum(pattern, matrices, state, precision=exact_result)]
    unnamed x22 -> x7, local copies, waits for them, and re-layouts: 0.77 us -> 9.38 us
    all_to_all x15 -> x0, local copies, waits for them, and re-layouts: 5.35 us -> none  [the longest x5 2.24 us: x_transposed(): lax.all_to_all(filtered, 'gx', split_axis=2, concat_axis=1, tiled=True)]
  transfers between devices with their start and end apart: 6 -> 0, of which waited for: 5 -> 0; matrix products, arithmetic and copies ran while one was open for 2% -> 0% of each run, Pallas kernels for 0% -> 0%
where the time goes in v1:
time: 57.1 us; the launch traced here: 56.7 us
  Pallas kernels  43.6 us (76%)
  local copies, waits for them, and re-layouts  10.6 us (19%)
  between operations  2.45 us (4%)
    pallas_call x1, Pallas kernels, shards(): pl.pallas_call(functools.partial(kernel, nx, ny), out_shape=(jax.ShapeDty...  43.6 us
    unnamed x7, local copies, waits for them, and re-layouts  9.38 us
    reshape x1, local copies, waits for them, and re-layouts, shards(): inv_var.reshape(1, -1)  1.27 us

profile of v1, /device:TPU:0, one launch (start us, length us, event | category | flops | bytes accessed | tf_op | source)
XLA Modules:
  0.0 56.7 jit_solution(5552071486925072148)
XLA Ops:
  0.6 1.3 %reshape.25.inv_var = f32[1,616]{1,0:T(1,128)} reshape(f32[616]{0:T(1024)} %param.19) | data formatting | bytes 4928 | tf_op jit(solution)/shard_map/reshape | solution.py:415
  1.9 1.9 %copy.16.innovation = f32[128,616]{1,0:T(8,128)} copy(f32[128,616]{0,1:T(8,128)} %param.16) | data formatting | bytes 630784 | tf_op args[5]
  3.8 2.8 %copy.15.jacobian = f32[4,128,616]{2,1,0:T(8,128)} copy(f32[4,128,616]{1,2,0:T(8,128)} %param.15) | data formatting | bytes 2523136 | tf_op args[4]
  6.5 43.6 %shard_map.138 = (f32[4,32,16,128]{3,2,1,0:T(8,128)}, f32[128,616]{1,0:T(8,128)}, f32[8,616]{1,0:T(8,128)}, f32[1,1]{1,0:T(1,128)}) custom-call(f32[4,32,16,128]{3,2,1,0:T(8,128)} %control.1, f32[4,128]{1,0:T(4,128)} %level_rate.1, f32[1,128]{1,0:T(1,128)} %bitcast.7, f32[1,128]{1,0:T(1,128)} %bitcast.8, f32[4,128,616]{2,1,0:T(8,128)} %copy.15.jacobian, ...), custom_call_target="tpu_custom_call" | custom-call | tf_op jit(solution)/shard_map/pallas_call | solution.py:382
  50.1 0.0 copy-start
  50.2 1.9 %copy.17 = f32[128,616]{0,1:T(8,128)} copy(f32[128,616]{1,0:T(8,128)} %get-tuple-element.13) | data formatting | bytes 630784
  52.0 2.3 %copy.21 = f32[4,32,16,128]{3,2,1,0:T(8,128)} copy(f32[4,32,16,128]{3,2,1,0:T(8,128)} %get-tuple-element.20) | data formatting | bytes 2097152
  54.3 0.0 copy-done
  54.3 0.6 %copy.22 = f32[8,616]{1,0:T(8,128)} copy(f32[8,616]{1,0:T(8,128)S(1)} %copy-done) | data formatting | bytes 39424
Async XLA Ops:
  50.1 4.2 %copy-start = (f32[8,616]{1,0:T(8,128)S(1)}, f32[8,616]{1,0:T(8,128)}, u32[]{:S(2)}) copy-start(f32[8,616]{1,0:T(8,128)} %get-tuple-element.22) | copy-start | bytes 59140

commit v2 on v1

--- a/solution.py
+++ b/solution.py
@@ -13,7 +13,7 @@
 CUT = -1e30
 
 X_ENDS, X_CORNER, X_CARRY, X_BACK_CORNER, X_BIAS = range(5)
-Y_CELLS, Y_ENDS, Y_CORNER, Y_PROF, Y_GRAD, Y_BIAS, Y_CARRY, Y_BACK_CORNER = range(8)
+Y_CELLS, Y_ENDS, Y_CORNER, Y_BASE, Y_DEP, Y_BIAS, Y_CARRY, Y_BACK_CORNER = range(8)
 
 
 def iota(shape, axis):
@@ -68,16 +68,16 @@
     cell_row, grad_out, dep_out, bias_out, cost_out,
     state, jac, innov, state_h, state_l, jf_h, jf_l, decay_x, decay_y, carry,
     x_send, x_recv, y_send, y_recv, c_send, c_recv, c2_send, c2_recv,
-    cells_send, cells_recv, prof_send, prof_recv, gsl_send, gsl_recv,
+    cells_send, cells_recv, base_send, base_recv, dsl_send, dsl_recv,
     bx_send, bx_recv, by_send, by_recv, bc_send, bc_recv, bc2_send, bc2_recv,
     b1_recv, b2_recv, b1_send, b2_send, local_sem, sx_sem, rx_sem, sy_sem, ry_sem,
 ):
     gx, gy = lax.axis_index("gx"), lax.axis_index("gy")
     variables, rows, cols, levels = control.shape
     cells = rows * cols
-    channels = innovation.shape[1]
-    obs = innovation.shape[0]
-    cap = prof_send.shape[1]
+    channels, obs = innovation.shape
+    cap = base_send.shape[1]
+    kinds = pred_t.shape[0]
     slots = ny * cap
     width = variables * levels
     ends = rows + cols + 8
@@ -128,11 +128,8 @@
     tile_c = to_col(tile_r)
     at0, at1 = iota((obs, obs), 0), iota((obs, obs), 1)
     same = tile_c == tile_r
-    rank_c = jnp.sum(jnp.where(same & (at1 < at0), 1.0, 0.0), axis=1, keepdims=True)
     rank_r = jnp.sum(jnp.where(same & (at0 < at1), 1.0, 0.0), axis=0, keepdims=True)
-    slot_c = (tile_c * cap + rank_c).astype(jnp.int32)
     slot_r = (tile_r * cap + rank_r).astype(jnp.int32)
-    placing = jnp.where(slot_c == iota((obs, slots), 1), 1.0, 0.0).astype(BF16)
     placed_t = slot_r == iota((slots, obs), 0)
     placing_t = jnp.where(placed_t, 1.0, 0.0).astype(BF16)
     sent = jnp.sum(jnp.where(placed_t, cell_r + 1.0, 0.0), axis=1, keepdims=True)
@@ -175,7 +172,8 @@
     e_parts = split(jnp.exp(e_log))
 
     pl.semaphore_wait(barrier, nx + ny - 2)
-    each(ny, gy, lambda t: y_copy(Y_CELLS, cells_send.at[t], cells_recv, t, gy).start(), other)
+    talk = each
+    talk(ny, gy, lambda t: y_copy(Y_CELLS, cells_send.at[t], cells_recv, t, gy).start(), other)
 
     loads[0].wait()
     for v in range(variables):
@@ -187,9 +185,21 @@
     x_send[...] = tails[0:rows]
     y_send[...] = tails[rows:rows + cols]
     c_send[...] = tails[rows + cols:rows + cols + 1]
-    each(nx, gx, lambda t: x_copy(X_CORNER, c_send, c_recv, t, gx).start(), later)
-    each(nx, gx, lambda t: x_copy(X_ENDS, x_send, x_recv, t, gx).start(), later)
-    each(ny, gy, lambda t: y_copy(Y_ENDS, y_send, y_recv, t, gy).start(), later)
+    talk(nx, gx, lambda t: x_copy(X_CORNER, c_send, c_recv, t, gx).start(), later)
+    talk(nx, gx, lambda t: x_copy(X_ENDS, x_send, x_recv, t, gx).start(), later)
+    talk(ny, gy, lambda t: y_copy(Y_ENDS, y_send, y_recv, t, gy).start(), later)
+
+    nn, nt, tn = ((1,), (0,)), ((1,), (1,)), ((0,), (0,))
+    loads[2].wait()
+    pred = split(pred_t[...])
+    base_parts = split(innov[...] - mm3(split(bias_coef[...]), pred, tn))
+    to_slots = lambda parts: mm(placing_t, parts[0], nt) + mm(placing_t, parts[1], nt)
+    base_send[:, :, 0:channels] = to_slots(base_parts).reshape(ny, cap, channels)
+    base_send[:, :, channels:channels + kinds] = to_slots(pred).reshape(ny, cap, kinds)
+    rest = base_send.shape[2] - channels - kinds
+    base_send[:, :, channels + kinds:] = jnp.zeros((ny, cap, rest), F32)
+    talk(ny, gy, lambda t: y_copy(Y_BASE, base_send.at[t], base_recv, t, gy).start(), other)
+    base_recv[gy] = base_send[gy]
 
     carry[...] = jnp.zeros_like(carry)
 
@@ -197,7 +207,7 @@
         row = ref[side, pl.ds(t, 1), :]
         return jnp.concatenate([row] * (width // 128), axis=1)
 
-    each(ny, gy, lambda t: y_copy(Y_CELLS, cells_send.at[t], cells_recv, t, t).wait_recv(), other)
+    talk(ny, gy, lambda t: y_copy(Y_CELLS, cells_send.at[t], cells_recv, t, t).wait_recv(), other)
     landed = cells_recv[...].reshape(slots, 128)[:, 0:1] - 1.0
     y_s = jnp.floor((landed + 0.5) * (1.0 / cols))
     x_s = (landed - y_s * cols).astype(jnp.int32)
@@ -222,9 +232,9 @@
         x_copy(X_CORNER, c_send, c_recv, t, t).wait_recv()
         carry[rows + cols:rows + cols + 1, :] += widen(decay_x, 0, t) * c_recv[t]
 
-    each(nx, gx, add_corner, earlier)
+    talk(nx, gx, add_corner, earlier)
     c2_send[...] = carry[rows + cols:rows + cols + 1, :]
-    each(ny, gy, lambda t: y_copy(Y_CORNER, c2_send, c2_recv, t, gy).start(), later)
+    talk(ny, gy, lambda t: y_copy(Y_CORNER, c2_send, c2_recv, t, gy).start(), later)
     carry[rows + cols:rows + cols + 1, :] = jnp.zeros((1, width), F32)
 
     prof = mm3(w_cells, field)
@@ -234,15 +244,11 @@
     m0, m1 = iota((levels, levels), 0), iota((levels, levels), 1)
     for v in range(variables):
         s_r, s_c = sums_both(l_log[v:v + 1, :], 0)
-        q_c = s_c - to_col(l_scale[v:v + 1, :])
-        f_t = split(jnp.exp(jnp.where(m0 <= m1, s_r - q_c, CUT)))
-        high, low = split(mm3(f_t, split(jac[v])))
-        jf_h[v * levels:(v + 1) * levels, :] = high
-        jf_l[v * levels:(v + 1) * levels, :] = low
-
-    loads[2].wait()
-    pred = split(pred_t[...])
-    base = innov[...] - mm3(pred, split(bias_coef[...]), ((0,), (0,)))
+        q_r = s_r - l_scale[v:v + 1, :]
+        f_v = split(jnp.exp(jnp.where(m1 <= m0, s_c - q_r, CUT)))
+        high, low = split(mm3(split(jac[v]), f_v))
+        jf_h[:, v * levels:(v + 1) * levels] = high
+        jf_l[:, v * levels:(v + 1) * levels] = low
 
     def add_x(t):
         x_copy(X_ENDS, x_send, x_recv, t, t).wait_recv()
@@ -256,48 +262,38 @@
         y_copy(Y_CORNER, c2_send, c2_recv, t, t).wait_recv()
         carry[rows + cols:rows + cols + 1, :] += widen(decay_y, 0, t) * c2_recv[t]
 
-    each(ny, gy, add_y, earlier)
-    each(nx, gx, add_x, earlier)
-    each(ny, gy, add_c2, earlier)
+    talk(ny, gy, add_y, earlier)
+    talk(nx, gx, add_x, earlier)
+    talk(ny, gy, add_c2, earlier)
     prof = prof + mm3(w_carry, split(carry[...]))
-    prof_send[...] = prof.reshape(ny, cap, width)
-    each(ny, gy, lambda t: y_copy(Y_PROF, prof_send.at[t], prof_recv, t, gy).start(), other)
-    prof_recv[gy] = prof_send[gy]
-    each(ny, gy, lambda t: y_copy(Y_PROF, prof_send.at[t], prof_recv, t, t).wait_recv(), other)
-
-    got_h, got_l = split(prof_recv[...].reshape(slots, width))
-    nn = ((1,), (0,))
-    own = (mm(placing, got_h, nn).astype(BF16), mm(placing, got_l, nn).astype(BF16))
+    talk(ny, gy, lambda t: y_copy(Y_BASE, base_send.at[t], base_recv, t, t).wait_recv(), other)
+    arrived = base_recv[...]
     jf = (jf_h[...], jf_l[...])
-    departures = base - mm3(own, jf)
-    dep_out[...] = departures
-    weighted = departures * inv_var[...]
+    departures = arrived[:, :, 0:channels].reshape(slots, channels) - mm3(split(prof), jf, nt)
+    dsl_send[...] = departures.reshape(ny, cap, channels)
+    weighted = departures * inv_var[...].reshape(1, channels)
     w_parts = split(weighted)
-    g_h, g_l = split(mm3(w_parts, jf, ((1,), (1,))))
-    gsl_send[...] = (mm(placing_t, g_h, nn) + mm(placing_t, g_l, nn)).reshape(ny, cap, width)
-    each(ny, gy, lambda t: y_copy(Y_GRAD, gsl_send.at[t], gsl_recv, t, gy).start(), other)
-    gsl_recv[gy] = gsl_send[gy]
-
-    b1_send[:, 0:channels] = -mm3(pred, w_parts)
-    cost = jnp.sum(jnp.sum(departures * weighted, axis=1, keepdims=True), axis=0, keepdims=True)
-    b1_send[:, channels:] = jnp.broadcast_to(0.5 * cost, (b1_send.shape[0], b1_send.shape[1] - channels))
-    each(ny, gy, lambda t: y_copy(Y_BIAS, b1_send, b1_recv, t, gy).start(), other)
-    b1_recv[gy] = b1_send[...]
-
-    each(ny, gy, lambda t: y_copy(Y_GRAD, gsl_send.at[t], gsl_recv, t, t).wait_recv(), other)
-    grads = split(gsl_recv[...].reshape(slots, width))
-    tn = ((0,), (0,))
+    grads = split(mm3(w_parts, jf))
     out = mm3(w_carry, grads, tn)
     bx_send[...] = out[0:rows]
     by_send[...] = out[rows:rows + cols]
     bc_send[...] = out[rows + cols:rows + cols + 1]
-    each(nx, gx, lambda t: x_copy(X_BACK_CORNER, bc_send, bc_recv, t, gx).start(), earlier)
-    each(nx, gx, lambda t: x_copy(X_CARRY, bx_send, bx_recv, t, gx).start(), earlier)
-    each(ny, gy, lambda t: y_copy(Y_CARRY, by_send, by_recv, t, gy).start(), earlier)
-
-    each(ny, gy, lambda t: y_copy(Y_BIAS, b1_send, b1_recv, t, t).wait_recv(), other)
+    talk(nx, gx, lambda t: x_copy(X_BACK_CORNER, bc_send, bc_recv, t, gx).start(), earlier)
+    talk(nx, gx, lambda t: x_copy(X_CARRY, bx_send, bx_recv, t, gx).start(), earlier)
+    talk(ny, gy, lambda t: y_copy(Y_CARRY, by_send, by_recv, t, gy).start(), earlier)
+
+    b1_send[:, 0:channels] = -mm3(split(arrived[:, :, channels:channels + kinds].reshape(slots, kinds)), w_parts, tn)
+    cost = jnp.sum(jnp.sum(departures * weighted, axis=1, keepdims=True), axis=0, keepdims=True)
+    b1_send[:, channels:] = jnp.broadcast_to(0.5 * cost, (b1_send.shape[0], b1_send.shape[1] - channels))
+    talk(ny, gy, lambda t: y_copy(Y_BIAS, b1_send, b1_recv, t, gy).start(), other)
+    b1_recv[gy] = b1_send[...]
+
+    talk(ny, gy, lambda t: y_copy(Y_DEP, dsl_send.at[t], dsl_recv, t, gy).start(), other)
+    dsl_recv[gy] = dsl_send[gy]
+
+    talk(ny, gy, lambda t: y_copy(Y_BIAS, b1_send, b1_recv, t, t).wait_recv(), other)
     b2_send[...] = jnp.sum(b1_recv[...], axis=0)
-    each(nx, gx, lambda t: x_copy(X_BIAS, b2_send, b2_recv, t, gx).start(), other)
+    talk(nx, gx, lambda t: x_copy(X_BIAS, b2_send, b2_recv, t, gx).start(), other)
     b2_recv[gx] = b2_send[...]
 
     carry[...] = jnp.zeros_like(carry)
@@ -306,12 +302,16 @@
         x_copy(X_BACK_CORNER, bc_send, bc_recv, t, t).wait_recv()
         carry[rows + cols:rows + cols + 1, :] += widen(decay_x, 1, t) * bc_recv[t]
 
-    each(nx, gx, back_corner, later)
+    talk(nx, gx, back_corner, later)
     bc2_send[...] = carry[rows + cols:rows + cols + 1, :]
-    each(ny, gy, lambda t: y_copy(Y_BACK_CORNER, bc2_send, bc2_recv, t, gy).start(), earlier)
+    talk(ny, gy, lambda t: y_copy(Y_BACK_CORNER, bc2_send, bc2_recv, t, gy).start(), earlier)
     carry[rows + cols:rows + cols + 1, :] = jnp.zeros((1, width), F32)
 
     here = mm3(w_cells, grads, tn)
+
+    talk(ny, gy, lambda t: y_copy(Y_DEP, dsl_send.at[t], dsl_recv, t, t).wait_recv(), other)
+    d_h, d_l = split(dsl_recv[...].reshape(slots, channels))
+    dep_out[...] = mm(d_h, placing_t, tn) + mm(d_l, placing_t, tn)
 
     def back_x(t):
         x_copy(X_CARRY, bx_send, bx_recv, t, t).wait_recv()
@@ -325,24 +325,24 @@
         y_copy(Y_BACK_CORNER, bc2_send, bc2_recv, t, t).wait_recv()
         carry[rows + cols:rows + cols + 1, :] += widen(decay_y, 1, t) * bc2_recv[t]
 
-    each(ny, gy, back_y, later)
-    each(nx, gx, back_x, later)
-    each(ny, gy, back_c2, later)
+    talk(ny, gy, back_y, later)
+    talk(nx, gx, back_x, later)
+    talk(ny, gy, back_c2, later)
     here = here + mm3(e_parts, split(carry[...]), tn)
     for v in range(variables):
         grad_out[v] = here[:, v * levels:(v + 1) * levels].reshape(rows, cols, levels)
 
-    each(nx, gx, lambda t: x_copy(X_BIAS, b2_send, b2_recv, t, t).wait_recv(), other)
+    talk(nx, gx, lambda t: x_copy(X_BIAS, b2_send, b2_recv, t, t).wait_recv(), other)
     summed = jnp.sum(b2_recv[...], axis=0)
     obs_total = obs * nx * ny
     bias_out[...] = summed[:, 0:channels] * obs_total ** -0.5
     cost_out[...] = summed[0:1, channels:channels + 1] * (1.0 / obs_total)
 
-    each(ny, gy, lambda t: y_copy(Y_CELLS, cells_send.at[t], cells_recv, t, gy).wait_send(), other)
-    each(ny, gy, lambda t: y_copy(Y_PROF, prof_send.at[t], prof_recv, t, gy).wait_send(), other)
-    each(ny, gy, lambda t: y_copy(Y_GRAD, gsl_send.at[t], gsl_recv, t, gy).wait_send(), other)
-    each(ny, gy, lambda t: y_copy(Y_BIAS, b1_send, b1_recv, t, gy).wait_send(), other)
-    each(nx, gx, lambda t: x_copy(X_BIAS, b2_send, b2_recv, t, gx).wait_send(), other)
+    talk(ny, gy, lambda t: y_copy(Y_CELLS, cells_send.at[t], cells_recv, t, gy).wait_send(), other)
+    talk(ny, gy, lambda t: y_copy(Y_BASE, base_send.at[t], base_recv, t, gy).wait_send(), other)
+    talk(ny, gy, lambda t: y_copy(Y_DEP, dsl_send.at[t], dsl_recv, t, gy).wait_send(), other)
+    talk(ny, gy, lambda t: y_copy(Y_BIAS, b1_send, b1_recv, t, gy).wait_send(), other)
+    talk(nx, gx, lambda t: x_copy(X_BIAS, b2_send, b2_recv, t, gx).wait_send(), other)
 
     def forward_x(t):
         x_copy(X_CORNER, c_send, c_recv, t, gx).wait_send()
@@ -360,16 +360,17 @@
         y_copy(Y_CARRY, by_send, by_recv, t, gy).wait_send()
         y_copy(Y_BACK_CORNER, bc2_send, bc2_recv, t, gy).wait_send()
 
-    each(nx, gx, forward_x, later)
-    each(ny, gy, forward_y, later)
-    each(nx, gx, backward_x, earlier)
-    each(ny, gy, backward_y, earlier)
+    talk(nx, gx, forward_x, later)
+    talk(ny, gy, forward_y, later)
+    talk(nx, gx, backward_x, earlier)
+    talk(ny, gy, backward_y, earlier)
 
 
 def shards(nx, ny, control, level_rate, x_rate, y_rate, jacobian, innovation, predictors, bias_coef, inv_var,
            obs_tile, obs_cell):
     variables, rows, cols, levels = control.shape
     obs, channels = innovation.shape
+    by_channel = jnp.swapaxes(jacobian, 1, 2)
     cells, width = rows * cols, variables * levels
     cap = obs // 4
     kinds = predictors.shape[1]
@@ -383,7 +384,7 @@
         functools.partial(kernel, nx, ny),
         out_shape=(
             jax.ShapeDtypeStruct(control.shape, F32),
-            jax.ShapeDtypeStruct(innovation.shape, F32),
+            jax.ShapeDtypeStruct((channels, obs), F32),
             jax.ShapeDtypeStruct((kinds, channels), F32),
             jax.ShapeDtypeStruct((1, 1), F32),
         ),
@@ -391,17 +392,17 @@
         out_specs=(vmem, vmem, vmem, vmem),
         scratch_shapes=[
             pltpu.VMEM(control.shape, F32),
-            pltpu.VMEM(jacobian.shape, F32),
-            pltpu.VMEM(innovation.shape, F32),
+            pltpu.VMEM(by_channel.shape, F32),
+            pltpu.VMEM((channels, obs), F32),
             pltpu.VMEM((cells, width), BF16),
             pltpu.VMEM((cells, width), BF16),
-            pltpu.VMEM((width, channels), BF16),
-            pltpu.VMEM((width, channels), BF16),
+            pltpu.VMEM((channels, width), BF16),
+            pltpu.VMEM((channels, width), BF16),
             pltpu.VMEM((2, nx, 128), F32),
             pltpu.VMEM((2, ny, 128), F32),
             pltpu.VMEM((ends, width), F32),
             *both(nx, rows, width), *both(ny, cols, width), *both(nx, 1, width), *both(ny, 1, width),
-            *slotted(128), *slotted(width), *slotted(width),
+            *slotted(128), *slotted(wide), *slotted(channels),
             *both(nx, rows, width), *both(ny, cols, width), *both(nx, 1, width), *both(ny, 1, width),
             pltpu.VMEM((ny, kinds, wide), F32), pltpu.VMEM((nx, kinds, wide), F32),
             pltpu.VMEM((kinds, wide), F32), pltpu.VMEM((kinds, wide), F32),
@@ -411,9 +412,9 @@
         ],
         compiler_params=pltpu.CompilerParams(
             collective_id=0, has_side_effects=True, vmem_limit_bytes=60 * 1024 * 1024),
-    )(control, level_rate, x_rate.reshape(1, -1), y_rate.reshape(1, -1), jacobian, innovation, predictors.T,
-      bias_coef, inv_var.reshape(1, -1), obs_tile.reshape(1, -1), obs_cell.reshape(1, -1))
-    return grad, dep, bias, cost[0, 0]
+    )(control, level_rate, x_rate.reshape(1, -1), y_rate.reshape(1, -1), by_channel, innovation.T, predictors.T,
+      bias_coef, inv_var, obs_tile.reshape(1, -1), obs_cell.reshape(1, -1))
+    return grad, dep.T, bias, cost[0, 0]
 
 
 def solution(mesh):

time: 57.1 us -> 44.8 us (0.78)
  local copies, waits for them, and re-layouts: 10.6 us -> 3.66 us
  Pallas kernels: 43.6 us -> 38.4 us
    unnamed x7, local copies, waits for them, and re-layouts: 9.38 us -> 3.66 us
    pallas_call x1, Pallas kernels: 43.6 us -> 38.4 us  [shards(): pl.pallas_call(functools.partial(kernel, nx, ny), out_shape=(jax.ShapeDty...]
    reshape x1 -> x0, local copies, waits for them, and re-layouts: 1.27 us -> none  [shards(): inv_var.reshape(1, -1)]
where the time goes in v2:
time: 44.8 us; the launch traced here: 44.5 us
  Pallas kernels  38.4 us (86%)
  local copies, waits for them, and re-layouts  3.66 us (8%)
  between operations  2.43 us (5%)
    pallas_call x1, Pallas kernels, shards(): pl.pallas_call(functools.partial(kernel, nx, ny), out_shape=(jax.ShapeDty...  38.4 us
    unnamed x7, local copies, waits for them, and re-layouts  3.66 us

profile of v2, /device:TPU:0, one launch (start us, length us, event | category | flops | bytes accessed | tf_op | source)
XLA Modules:
  0.0 44.5 jit_solution(17841750307852035353)
XLA Ops:
  0.6 38.4 %shard_map.138 = (f32[4,32,16,128]{3,2,1,0:T(8,128)}, f32[616,128]{1,0:T(8,128)}, f32[8,616]{1,0:T(8,128)}, f32[1,1]{1,0:T(1,128)}) custom-call(f32[4,32,16,128]{3,2,1,0:T(8,128)} %control.1, f32[4,128]{1,0:T(4,128)} %level_rate.1, f32[1,128]{1,0:T(1,128)} %bitcast.13, f32[1,128]{1,0:T(1,128)} %bitcast.14, f32[4,616,128]{2,1,0:T(8,128)} %bitcast.9, ...), custom_call_target="tpu_custom_call" | custom-call | tf_op jit(solution)/shard_map/pallas_call | solution.py:383
  39.1 0.0 copy-start
  39.1 0.0 copy-start.1
  39.1 2.3 %copy.19 = f32[4,32,16,128]{3,2,1,0:T(8,128)} copy(f32[4,32,16,128]{3,2,1,0:T(8,128)} %get-tuple-element.16) | data formatting | bytes 2097152
  41.4 0.0 copy-done
  41.4 0.7 %copy.20 = f32[128,616]{0,1:T(8,128)} copy(f32[128,616]{0,1:T(8,128)S(1)} %bitcast.10) | data formatting | bytes 630784
  42.2 0.0 copy-done.1
  42.2 0.6 %copy.21 = f32[8,616]{1,0:T(8,128)} copy(f32[8,616]{1,0:T(8,128)S(1)} %copy-done.1) | data formatting | bytes 39424
Async XLA Ops:
  39.1 2.4 %copy-start = (f32[616,128]{1,0:T(8,128)S(1)}, f32[616,128]{1,0:T(8,128)}, u32[]{:S(2)}) copy-start(f32[616,128]{1,0:T(8,128)} %get-tuple-element.9) | copy-start | bytes 946180
  39.1 3.1 %copy-start.1 = (f32[8,616]{1,0:T(8,128)S(1)}, f32[8,616]{1,0:T(8,128)}, u32[]{:S(2)}) copy-start(f32[8,616]{1,0:T(8,128)} %get-tuple-element.18) | copy-start | bytes 59140

commit v3 on v2

--- a/solution.py
+++ b/solution.py
@@ -13,7 +13,7 @@
 CUT = -1e30
 
 X_ENDS, X_CORNER, X_CARRY, X_BACK_CORNER, X_BIAS = range(5)
-Y_CELLS, Y_ENDS, Y_CORNER, Y_BASE, Y_DEP, Y_BIAS, Y_CARRY, Y_BACK_CORNER = range(8)
+Y_CELLS, Y_ENDS, Y_CORNER, Y_BASE, Y_PROF, Y_BIAS, Y_CARRY, Y_BACK_CORNER = range(8)
 
 
 def iota(shape, axis):
@@ -68,7 +68,7 @@
     cell_row, grad_out, dep_out, bias_out, cost_out,
     state, jac, innov, state_h, state_l, jf_h, jf_l, decay_x, decay_y, carry,
     x_send, x_recv, y_send, y_recv, c_send, c_recv, c2_send, c2_recv,
-    cells_send, cells_recv, base_send, base_recv, dsl_send, dsl_recv,
+    cells_send, cells_recv, base_send, base_recv, prof_send, prof_recv,
     bx_send, bx_recv, by_send, by_recv, bc_send, bc_recv, bc2_send, bc2_recv,
     b1_recv, b2_recv, b1_send, b2_send, local_sem, sx_sem, rx_sem, sy_sem, ry_sem,
 ):
@@ -87,8 +87,8 @@
         pltpu.make_async_copy(jacobian, jac, local_sem.at[1]),
         pltpu.make_async_copy(innovation, innov, local_sem.at[2]),
     ]
-    for load in loads:
-        load.start()
+    for at in (2, 0, 1):
+        loads[at].start()
 
     barrier = pltpu.get_barrier_semaphore()
 
@@ -136,6 +136,23 @@
     cells_send[...] = jnp.broadcast_to(sent, (slots, 128)).reshape(ny, cap, 128)
     cells_recv[gy] = cells_send[gy]
 
+    nn, nt, tn = ((1,), (0,)), ((1,), (1,)), ((0,), (0,))
+    loads[2].wait()
+    pred = split(pred_t[...])
+    base = innov[...] - mm3(split(bias_coef[...]), pred, tn)
+    base_parts = split(base)
+    to_slots = lambda parts: mm(placing_t, parts[0], nt) + mm(placing_t, parts[1], nt)
+    base_send[:, :, 0:channels] = to_slots(base_parts).reshape(ny, cap, channels)
+    base_send[:, :, channels:channels + kinds] = to_slots(pred).reshape(ny, cap, kinds)
+    rest = base_send.shape[2] - channels - kinds
+    base_send[:, :, channels + kinds:] = jnp.zeros((ny, cap, rest), F32)
+    pl.semaphore_wait(barrier, nx + ny - 2)
+    talk = each
+    talk(ny, gy, lambda t: y_copy(Y_CELLS, cells_send.at[t], cells_recv, t, gy).start(), other)
+    talk(ny, gy, lambda t: y_copy(Y_BASE, base_send.at[t], base_recv, t, gy).start(), other)
+    base_recv[gy] = base_send[gy]
+    innov[...] = base
+
     x_log, x_scale = logs(x_rate[...])
     y_log, y_scale = logs(y_rate[...])
     fwd, bwd = between(x_log, gx, nx, cols)
@@ -170,10 +187,6 @@
     to_x, to_y = t_x - qx_n, t_y - qy_n
     e_log = jnp.where(on_x, to_x, jnp.where(on_y, to_y, jnp.where(e == rows + cols, to_x + to_y, CUT)))
     e_parts = split(jnp.exp(e_log))
-
-    pl.semaphore_wait(barrier, nx + ny - 2)
-    talk = each
-    talk(ny, gy, lambda t: y_copy(Y_CELLS, cells_send.at[t], cells_recv, t, gy).start(), other)
 
     loads[0].wait()
     for v in range(variables):
@@ -189,18 +202,6 @@
     talk(nx, gx, lambda t: x_copy(X_ENDS, x_send, x_recv, t, gx).start(), later)
     talk(ny, gy, lambda t: y_copy(Y_ENDS, y_send, y_recv, t, gy).start(), later)
 
-    nn, nt, tn = ((1,), (0,)), ((1,), (1,)), ((0,), (0,))
-    loads[2].wait()
-    pred = split(pred_t[...])
-    base_parts = split(innov[...] - mm3(split(bias_coef[...]), pred, tn))
-    to_slots = lambda parts: mm(placing_t, parts[0], nt) + mm(placing_t, parts[1], nt)
-    base_send[:, :, 0:channels] = to_slots(base_parts).reshape(ny, cap, channels)
-    base_send[:, :, channels:channels + kinds] = to_slots(pred).reshape(ny, cap, kinds)
-    rest = base_send.shape[2] - channels - kinds
-    base_send[:, :, channels + kinds:] = jnp.zeros((ny, cap, rest), F32)
-    talk(ny, gy, lambda t: y_copy(Y_BASE, base_send.at[t], base_recv, t, gy).start(), other)
-    base_recv[gy] = base_send[gy]
-
     carry[...] = jnp.zeros_like(carry)
 
     def widen(ref, side, t):
@@ -266,11 +267,14 @@
     talk(nx, gx, add_x, earlier)
     talk(ny, gy, add_c2, earlier)
     prof = prof + mm3(w_carry, split(carry[...]))
+    prof_send[...] = prof.reshape(ny, cap, width)
+    talk(ny, gy, lambda t: y_copy(Y_PROF, prof_send.at[t], prof_recv, t, gy).start(), other)
+    prof_recv[gy] = prof_send[gy]
+
     talk(ny, gy, lambda t: y_copy(Y_BASE, base_send.at[t], base_recv, t, t).wait_recv(), other)
     arrived = base_recv[...]
     jf = (jf_h[...], jf_l[...])
     departures = arrived[:, :, 0:channels].reshape(slots, channels) - mm3(split(prof), jf, nt)
-    dsl_send[...] = departures.reshape(ny, cap, channels)
     weighted = departures * inv_var[...].reshape(1, channels)
     w_parts = split(weighted)
     grads = split(mm3(w_parts, jf))
@@ -288,9 +292,6 @@
     talk(ny, gy, lambda t: y_copy(Y_BIAS, b1_send, b1_recv, t, gy).start(), other)
     b1_recv[gy] = b1_send[...]
 
-    talk(ny, gy, lambda t: y_copy(Y_DEP, dsl_send.at[t], dsl_recv, t, gy).start(), other)
-    dsl_recv[gy] = dsl_send[gy]
-
     talk(ny, gy, lambda t: y_copy(Y_BIAS, b1_send, b1_recv, t, t).wait_recv(), other)
     b2_send[...] = jnp.sum(b1_recv[...], axis=0)
     talk(nx, gx, lambda t: x_copy(X_BIAS, b2_send, b2_recv, t, gx).start(), other)
@@ -309,9 +310,10 @@
 
     here = mm3(w_cells, grads, tn)
 
-    talk(ny, gy, lambda t: y_copy(Y_DEP, dsl_send.at[t], dsl_recv, t, t).wait_recv(), other)
-    d_h, d_l = split(dsl_recv[...].reshape(slots, channels))
-    dep_out[...] = mm(d_h, placing_t, tn) + mm(d_l, placing_t, tn)
+    talk(ny, gy, lambda t: y_copy(Y_PROF, prof_send.at[t], prof_recv, t, t).wait_recv(), other)
+    back_parts = split(prof_recv[...].reshape(slots, width))
+    own = tuple(mm(placing_t, part, tn).astype(BF16) for part in back_parts)
+    dep_out[...] = innov[...] - mm3(jf, own, nt)
 
     def back_x(t):
         x_copy(X_CARRY, bx_send, bx_recv, t, t).wait_recv()
@@ -340,7 +342,7 @@
 
     talk(ny, gy, lambda t: y_copy(Y_CELLS, cells_send.at[t], cells_recv, t, gy).wait_send(), other)
     talk(ny, gy, lambda t: y_copy(Y_BASE, base_send.at[t], base_recv, t, gy).wait_send(), other)
-    talk(ny, gy, lambda t: y_copy(Y_DEP, dsl_send.at[t], dsl_recv, t, gy).wait_send(), other)
+    talk(ny, gy, lambda t: y_copy(Y_PROF, prof_send.at[t], prof_recv, t, gy).wait_send(), other)
     talk(ny, gy, lambda t: y_copy(Y_BIAS, b1_send, b1_recv, t, gy).wait_send(), other)
     talk(nx, gx, lambda t: x_copy(X_BIAS, b2_send, b2_recv, t, gx).wait_send(), other)
 
@@ -402,7 +404,7 @@
             pltpu.VMEM((2, ny, 128), F32),
             pltpu.VMEM((ends, width), F32),
             *both(nx, rows, width), *both(ny, cols, width), *both(nx, 1, width), *both(ny, 1, width),
-            *slotted(128), *slotted(wide), *slotted(channels),
+            *slotted(128), *slotted(wide), *slotted(width),
             *both(nx, rows, width), *both(ny, cols, width), *both(nx, 1, width), *both(ny, 1, width),
             pltpu.VMEM((ny, kinds, wide), F32), pltpu.VMEM((nx, kinds, wide), F32),
             pltpu.VMEM((kinds, wide), F32), pltpu.VMEM((kinds, wide), F32),

time: 44.8 us -> 45.8 us (1.022)
  Pallas kernels: 38.4 us -> 39.5 us
    pallas_call x1, Pallas kernels: 38.4 us -> 39.5 us  [shards(): pl.pallas_call(functools.partial(kernel, nx, ny), out_shape=(jax.ShapeDty...]
where the time goes in v3:
time: 45.8 us; the launch traced here: 45.6 us
  Pallas kernels  39.5 us (86%)
  local copies, waits for them, and re-layouts  3.66 us (8%)
  between operations  2.43 us (5%)
    pallas_call x1, Pallas kernels, shards(): pl.pallas_call(functools.partial(kernel, nx, ny), out_shape=(jax.ShapeDty...  39.5 us
    unnamed x7, local copies, waits for them, and re-layouts  3.66 us

profile of v3, /device:TPU:0, one launch (start us, length us, event | category | flops | bytes accessed | tf_op | source)
XLA Modules:
  0.0 45.6 jit_solution(7835093502823536317)
XLA Ops:
  0.6 39.5 %shard_map.138 = (f32[4,32,16,128]{3,2,1,0:T(8,128)}, f32[616,128]{1,0:T(8,128)}, f32[8,616]{1,0:T(8,128)}, f32[1,1]{1,0:T(1,128)}) custom-call(f32[4,32,16,128]{3,2,1,0:T(8,128)} %control.1, f32[4,128]{1,0:T(4,128)} %level_rate.1, f32[1,128]{1,0:T(1,128)} %bitcast.13, f32[1,128]{1,0:T(1,128)} %bitcast.14, f32[4,616,128]{2,1,0:T(8,128)} %bitcast.9, ...), custom_call_target="tpu_custom_call" | custom-call | tf_op jit(solution)/shard_map/pallas_call | solution.py:385
  40.1 0.0 copy-start
  40.1 0.0 copy-start.1
  40.1 2.3 %copy.19 = f32[4,32,16,128]{3,2,1,0:T(8,128)} copy(f32[4,32,16,128]{3,2,1,0:T(8,128)} %get-tuple-element.16) | data formatting | bytes 2097152
  42.5 0.0 copy-done
  42.5 0.7 %copy.20 = f32[128,616]{0,1:T(8,128)} copy(f32[128,616]{0,1:T(8,128)S(1)} %bitcast.10) | data formatting | bytes 630784
  43.2 0.0 copy-done.1
  43.2 0.6 %copy.21 = f32[8,616]{1,0:T(8,128)} copy(f32[8,616]{1,0:T(8,128)S(1)} %copy-done.1) | data formatting | bytes 39424
Async XLA Ops:
  40.1 2.4 %copy-start = (f32[616,128]{1,0:T(8,128)S(1)}, f32[616,128]{1,0:T(8,128)}, u32[]{:S(2)}) copy-start(f32[616,128]{1,0:T(8,128)} %get-tuple-element.9) | copy-start | bytes 946180
  40.1 3.1 %copy-start.1 = (f32[8,616]{1,0:T(8,128)S(1)}, f32[8,616]{1,0:T(8,128)}, u32[]{:S(2)}) copy-start(f32[8,616]{1,0:T(8,128)} %get-tuple-element.18) | copy-start | bytes 59140
